TPU v7x, 32 devices: a whole 2x2x4 slice. The times are simulated.
32 devices in a mesh: head: 4 (over y, x), seq: 8 (over z, core).
Axes of the slice: x: 2, y: 2, z: 4, core: 2. Of those that a mesh axis runs over, the one named last changes fastest.
Arguments:
- queries: bfloat16 [8, 64, 576], P('seq', 'head'), may hold values from -400 to 400
- query_pos: int32 [8], replicated, may hold values from 2019 to 2047, as said below
- latents: bfloat16 [2048, 576], P('seq'), may hold values from -6 to 6
- valid_keys: int32 [8], P('seq'), may hold values from 128 to 256, as said below
- output_gradient: bfloat16 [8, 64, 512], P('seq', 'head'), may hold values from -600 to 600
- kv_down: bfloat16 [7168, 576], P('head'), may hold values from -0.0625 to 0.0625
Outputs:
- latent_grad: float32 [2048, 576], P('seq')
- input_grad: bfloat16 [2048, 7168], P('seq', 'head')
Inputs may be any that keep to these rules, and one draw needn't show every extreme that they name: `query_pos`: positions rise strictly with the query index, consecutive ones differ by 1 to 4, and the last is 2047. The first valid_keys[s] positions of shard s are valid; some shard is full and some holds exactly half.
All inputs are finite; a program needn't handle non-finite values.
Results may differ from a plain program's by a relative error of at most 0.015.
Values may be sent and summed in bfloat16 or wider, within the bound.
No kernel may reach another device: no remote copies, remote signals or barrier semaphores. Data moves between devices by JAX's collectives and lax.ppermute only.
A program may use at most 64 MiB of HBM per device.

v0:
```python
import jax
import jax.numpy as jnp
from jax import lax
from jax.sharding import PartitionSpec as P

score_scale = 192.0 ** (-0.5)


def combined_all(value, axis, join):
    pieces = jax.tree.map(lambda part: lax.all_gather(part, axis), value)
    head = jax.tree.map(lambda part: part[0], pieces)
    tail = jax.tree.map(lambda part: part[1:], pieces)
    so_far, _ = lax.scan(lambda so_far, share: (join(so_far, share), None), head, tail)
    return so_far


def join_totals(first_part, second_part):
    top = jnp.maximum(first_part[0], second_part[0])
    first_weight = jnp.exp(first_part[0] - top)
    second_weight = jnp.exp(second_part[0] - top)
    return (top, first_part[1] * first_weight + second_part[1] * second_weight)


def shards(queries, query_pos, latents, valid_keys, output_gradient, kv_down):
    key_count = latents.shape[0]
    latent_span = output_gradient.shape[2]
    all_query, gradient_total = (
        lax.all_gather(queries, "seq", axis=0, tiled=True),
        lax.all_gather(output_gradient, "seq", axis=0, tiled=True),
    )
    first_key = lax.axis_index("seq") * key_count
    local_index = jnp.arange(key_count, dtype=jnp.int32)
    key_pos = first_key + local_index
    visible = (local_index < valid_keys[0])[None, :] & (key_pos[None, :] <= query_pos[:, None])
    visible = visible[:, None, :]
    scores = (
        jnp.einsum("qhc,kc->qhk", all_query, latents, preferred_element_type=jnp.float32)
        * score_scale
    )
    scores = jnp.where(visible, scores, -1e30)
    local_max = jnp.max(scores, axis=-1)
    shifted = jnp.where(visible, jnp.exp(scores - local_max[..., None]), 0.0)
    local_total = jnp.sum(shifted, axis=-1)
    dprobs = jnp.einsum(
        "mcg,dg->mcd", gradient_total, latents[:, :latent_span], preferred_element_type=jnp.float32
    )
    row_max, row_total = combined_all((local_max, local_total), "seq", join_totals)
    lse = row_max + jnp.log(row_total)
    probs = jnp.where(visible, jnp.exp(scores - lse[..., None]), 0.0)
    delta_rows = lax.psum(jnp.sum(probs * dprobs, axis=-1), "seq")
    dscores = probs * (dprobs - delta_rows[..., None])
    probs_b = probs.astype(jnp.bfloat16)
    dscores_b = dscores.astype(jnp.bfloat16)
    key_contribution = (
        jnp.einsum("qhk,qhc->kc", dscores_b, all_query, preferred_element_type=jnp.float32)
        * score_scale
    )
    value_contribution = jnp.einsum(
        "qhk,qhv->kv", probs_b, gradient_total, preferred_element_type=jnp.float32
    )
    owned = lax.psum_scatter(
        jnp.concatenate(
            [
                key_contribution[:, :latent_span] + value_contribution,
                key_contribution[:, latent_span:],
            ],
            axis=1,
        ).astype(jnp.bfloat16),
        "head",
        scatter_dimension=0,
        tiled=True,
    ).astype(jnp.float32)
    latent_grad = lax.all_gather(owned.astype(jnp.bfloat16), "head", axis=0, tiled=True).astype(
        owned.dtype
    )
    input_grad = lax.dot_general(
        latent_grad.astype(jnp.bfloat16),
        kv_down,
        (((1,), (1,)), ((), ())),
        preferred_element_type=jnp.float32,
    ).astype(jnp.bfloat16)
    return (latent_grad, input_grad)


def solution(mesh):
    placed = (
        P("seq", "head", None),
        P(),
        P("seq", None),
        P("seq"),
        P("seq", "head", None),
        P("head", None),
    )
    return jax.shard_map(
        shards,
        mesh=mesh,
        in_specs=placed,
        out_specs=(P("seq", None), P("seq", "head")),
        check_vma=False,
    )
```

profile of v0, /device:TPU:0, one launch (start us, length us, event | category | flops | bytes accessed | tf_op | source)
XLA Modules:
  0.0 130.2 jit_solution(3458385779859424649)
XLA Ops:
  7.2 0.0 copy-start
  7.2 0.0 reduce-scatter.4.cloned.1.call-start
  8.0 15.9 %all_gather.21 = bf16[8,16,576]{2,1,0:T(8,128)(2,1)S(1)} all-gather(bf16[1,16,576]{2,1,0:T(8,128)(2,1)} %param.8), channel_id=1, replica_groups=mesh['head'=4,'seq'=8] {'seq'}, dimensions={0}, use_global_device_ids=true | all-gather | bytes 165888 | tf_op jit(solution)/shard_map/all_gather | solution.py:28
  24.0 0.7 compare_and_fusion
  24.7 1.2 fusion.21
  26.0 14.1 %all-gather = f32[64,16]{1,0:T(8,128)S(1)} all-gather(f32[8,16]{1,0:T(8,128)S(1)} %get-tuple-element.46), channel_id=2, replica_groups=mesh['head'=4,'seq'=8] {'seq'}, dimensions={0}, use_global_device_ids=true | all-gather | bytes 4608 | tf_op jit(solution)/shard_map/all_gather | solution.py:10
  40.1 0.2 select_reduce_fusion
  40.2 14.1 %all-gather.1 = f32[64,16]{1,0:T(8,128)S(1)} all-gather(f32[8,16]{1,0:T(8,128)S(1)} %select_reduce_fusion), channel_id=3, replica_groups=mesh['head'=4,'seq'=8] {'seq'}, dimensions={0}, use_global_device_ids=true | all-gather | bytes 4608 | tf_op jit(solution)/shard_map/all_gather | solution.py:10
  54.3 14.2 %all_gather.26 = bf16[8,16,512]{2,1,0:T(8,128)(2,1)S(1)} all-gather(bf16[1,16,512]{2,1,0:T(8,128)(2,1)} %param.12), channel_id=1, replica_groups=mesh['head'=4,'seq'=8] {'seq'}, dimensions={0}, use_global_device_ids=true | all-gather | bytes 147456 | tf_op jit(solution)/shard_map/all_gather | solution.py:29
  68.5 0.2 while.12
  68.8 1.2 multiply_reduce_fusion
  70.0 16.9 %psum.7 = f32[8,16]{1,0:T(8,128)S(1)} all-reduce(f32[8,16]{1,0:T(8,128)S(1)} %get-tuple-element.48), channel_id=1, replica_groups=mesh['head'=4,'seq'=8] {'seq'}, use_global_device_ids=true, to_apply=%region_5.6 | all-reduce | flops 128 | bytes 1024 | tf_op jit(solution)/shard_map/psum | solution.py:50
  86.9 0.3 fusion.2
  87.2 0.3 fusion.4
  87.6 0.9 copy.16
  88.5 0.0 reduce-scatter.4.cloned.1.call-update
  88.5 22.9 %reduce-scatter.4.cloned.1.call-done = bf16[64,576]{1,0:T(8,128)(2,1)} async-done(((bf16[256,576]{1,0:T(8,128)(2,1)}), bf16[64,576]{1,0:T(8,128)(2,1)}) %reduce-scatter.4.cloned.1.call-update) | async-done | bytes 73744 | tf_op jit(solution)/shard_map/reduce_scatter | solution.py:61
  111.4 9.2 %all_gather.27 = bf16[256,576]{1,0:T(8,128)(2,1)S(1)} all-gather(bf16[64,576]{1,0:T(8,128)(2,1)} %reduce-scatter.4.cloned.1.call-done), channel_id=1, replica_groups=mesh['head'=4,'seq'=8] {'head'}, dimensions={0}, use_global_device_ids=true | all-gather | bytes 368640 | tf_op jit(solution)/shard_map/all_gather | solution.py:73
  120.6 1.0 copy.13
  121.6 0.0 copy-done
  121.6 1.8 %convolution_convert_fusion = bf16[256,1792]{1,0:T(8,128)(2,1)} fusion(bf16[256,576]{1,0:T(8,128)(2,1)S(1)} %all_gather.27, bf16[1792,576]{0,1:T(8,128)(2,1)S(1)} %copy-done), kind=kOutput, calls=%fused_computation.5 | convolution fusion | flops 528941056 | bytes 3276800 | tf_op jit(solution)/shard_map/dot_general | solution.py:76
  (16 shorter events, 0.2 us)
Async XLA Ops:
  7.2 114.4 %copy-start = (bf16[1792,576]{0,1:T(8,128)(2,1)S(1)}, bf16[1792,576]{0,1:T(8,128)(2,1)}, u32[]{:S(2)}) copy-start(bf16[1792,576]{0,1:T(8,128)(2,1)} %param.13) | copy-start | bytes 6193156
  7.2 104.2 %reduce-scatter.4.cloned.1.call-start = ((), (), s32[]{:S(2)}) async-start(), calls=%async_computation.1 | async-start | bytes 409600 | tf_op jit(solution)/shard_map/reduce_scatter | solution.py:61
Sparse Core Ops, SparseCore 0:
  88.6 22.7 reduce-scatter.3
where the time goes:
time: 131 us; the launch traced here: 130 us
  blocking collectives  84.4 us (64%)
  waiting for transfers between devices  22.9 us (17%)
  between operations  14.9 us (11%)
  matrix products  4.91 us (4%)
  local copies, waits for them, and re-layouts  1.9 us (1%)
    all_gather x2, blocking collectives, combined_all(): pieces = jax.tree.map(lambda part: lax.all_gather(part, axis), value)  28.2 us
    reduce_scatter x1, waiting for transfers between devices, shards(): lax.psum_scatter(jnp.concatenate([key_contribution[:, :latent_span] + val...  22.9 us
    psum x1, blocking collectives, shards(): delta_rows = lax.psum(jnp.sum(probs * dprobs, axis=-1), 'seq')  16.9 us
    all_gather x1, blocking collectives, shards(): lax.all_gather(queries, 'seq', axis=0, tiled=True)  15.9 us
    all_gather x1, blocking collectives, shards(): lax.all_gather(output_gradient, 'seq', axis=0, tiled=True)  14.2 us
    all_gather x1, blocking collectives, shards(): lax.all_gather(owned.astype(jnp.bfloat16), 'head', axis=0, tiled=True)  9.19 us
  transfers between devices with their start and end apart: 1, of which 1 were waited for; matrix products, arithmetic and copies ran while one was open for 0% of the time, Pallas kernels for 0%

commit v1 on v0

--- a/solution.py
+++ b/solution.py
@@ -4,6 +4,11 @@
 from jax.sharding import PartitionSpec as P
 
 score_scale = 192.0 ** (-0.5)
+
+
+def gather_over(x, axis, along):
+    repeated = jnp.stack([x] * lax.axis_size(axis))
+    return jnp.concatenate(lax.all_to_all(repeated, axis, 0, 0), axis=along)
 
 
 def combined_all(value, axis, join):
@@ -25,7 +30,7 @@
     key_count = latents.shape[0]
     latent_span = output_gradient.shape[2]
     all_query, gradient_total = (
-        lax.all_gather(queries, "seq", axis=0, tiled=True),
+        gather_over(queries, "seq", 0),
         lax.all_gather(output_gradient, "seq", axis=0, tiled=True),
     )
     first_key = lax.axis_index("seq") * key_count

time: 131 us -> 123 us (0.939)
  blocking collectives: 84.4 us -> 68.8 us
  starting transfers between devices: 0.04 us -> 6.39 us
  local copies, waits for them, and re-layouts: 1.9 us -> 3.46 us
    all_gather x1 -> x0, blocking collectives: 15.9 us -> none  [shards(): lax.all_gather(queries, 'seq', axis=0, tiled=True)]
    all_to_all x0 -> x1, starting transfers between devices: none -> 6.35 us  [gather_over(): return jnp.concatenate(lax.all_to_all(repeated, axis, 0, 0), axis=along)]
    another operation x0 -> x1, local copies, waits for them, and re-layouts: none -> 1.55 us  [gather_over(): repeated = jnp.stack([x] * lax.axis_size(axis))]
  transfers between devices with their start and end apart: 1 -> 2, of which waited for: 1 -> 1; matrix products, arithmetic and copies ran while one was open for 0% -> 1% of each run, Pallas kernels for 0% -> 0%
where the time goes in v1:
time: 123 us; the launch traced here: 122 us
  blocking collectives  68.8 us (56%)
  waiting for transfers between devices  22.9 us (19%)
  between operations  14.8 us (12%)
  starting transfers between devices  6.39 us (5%)
  matrix products  4.9 us (4%)
  local copies, waits for them, and re-layouts  3.46 us (3%)
    all_gather x2, blocking collectives, combined_all(): pieces = jax.tree.map(lambda part: lax.all_gather(part, axis), value)  28.2 us
    reduce_scatter x1, waiting for transfers between devices, shards(): lax.psum_scatter(jnp.concatenate([key_contribution[:, :latent_span] + val...  22.9 us
    psum x1, blocking collectives, shards(): delta_rows = lax.psum(jnp.sum(probs * dprobs, axis=-1), 'seq')  16.4 us
    all_gather x1, blocking collectives, shards(): lax.all_gather(output_gradient, 'seq', axis=0, tiled=True)  15 us
    all_gather x1, blocking collectives, shards(): lax.all_gather(owned.astype(jnp.bfloat16), 'head', axis=0, tiled=True)  9.18 us
    all_to_all x1, starting transfers between devices, gather_over(): return jnp.concatenate(lax.all_to_all(repeated, axis, 0, 0), axis=along)  6.35 us
  transfers between devices with their start and end apart: 2, of which 1 were waited for; matrix products, arithmetic and copies ran while one was open for 1% of the time, Pallas kernels for 0%

profile of v1, /device:TPU:0, one launch (start us, length us, event | category | flops | bytes accessed | tf_op | source)
XLA Modules:
  0.0 122.4 jit_solution(11645397014605072411)
XLA Ops:
  7.2 0.0 copy-start
  7.2 1.6 %stack.2 = bf16[8,1,16,576]{3,2,1,0:T(8,128)(2,1)} broadcast(bf16[16,576]{1,0:T(8,128)(2,1)} %bitcast.54), dimensions={2,3} | broadcast | bytes 165888 | tf_op jit(solution)/shard_map/stack | solution.py:10
  8.7 6.4 %all-to-all-start = ((bf16[8,1,16,576]{3,2,1,0:T(8,128)(2,1)}), bf16[8,1,16,576]{3,2,1,0:T(8,128)(2,1)S(1)}, u32[]{:S(2)}, u32[]{:S(2)}) async-start(bf16[8,1,16,576]{3,2,1,0:T(8,128)(2,1)} %stack.2), calls=%async_computation | async-start | bytes 327680 | tf_op jit(solution)/shard_map/all_to_all | solution.py:11
  15.1 0.0 reduce-scatter.4.cloned.1.call-start
  15.8 15.0 %all_gather.22 = bf16[8,16,512]{2,1,0:T(8,128)(2,1)S(1)} all-gather(bf16[1,16,512]{2,1,0:T(8,128)(2,1)} %param.12), channel_id=1, replica_groups=mesh['head'=4,'seq'=8] {'seq'}, dimensions={0}, use_global_device_ids=true | all-gather | bytes 147456 | tf_op jit(solution)/shard_map/all_gather | solution.py:34
  30.8 0.7 compare_and_fusion
  31.6 0.0 all-to-all-done
  31.6 1.2 %fusion.23 = (f32[8,16]{1,0:T(8,128)S(1)}, f32[8,16,256]{2,1,0:T(8,128)S(1)}) fusion(bf16[256,576]{0,1:T(8,128)(2,1)} %param.10, bf16[8,1,16,576]{3,2,1,0:T(8,128)(2,1)S(1)} %all-to-all-done, pred[8,256]{1,0:T(8,128)(4,1)S(1)} %compare_and_fusion), kind=kOutput, calls=%fused_computation.41 | convolution fusion | flops 37846912 | bytes 576000 | tf_op jit(solution)/shard_map/qhc,kc->qhk/dot_general | solution.py:42
  32.8 14.1 %all-gather = f32[64,16]{1,0:T(8,128)S(1)} all-gather(f32[8,16]{1,0:T(8,128)S(1)} %get-tuple-element.46), channel_id=2, replica_groups=mesh['head'=4,'seq'=8] {'seq'}, dimensions={0}, use_global_device_ids=true | all-gather | bytes 4608 | tf_op jit(solution)/shard_map/all_gather | solution.py:15
  46.9 0.2 select_reduce_fusion
  47.1 14.1 %all-gather.1 = f32[64,16]{1,0:T(8,128)S(1)} all-gather(f32[8,16]{1,0:T(8,128)S(1)} %select_reduce_fusion), channel_id=3, replica_groups=mesh['head'=4,'seq'=8] {'seq'}, dimensions={0}, use_global_device_ids=true | all-gather | bytes 4608 | tf_op jit(solution)/shard_map/all_gather | solution.py:15
  61.2 0.2 while.12
  61.5 1.2 multiply_reduce_fusion
  62.7 16.4 %psum.7 = f32[8,16]{1,0:T(8,128)S(1)} all-reduce(f32[8,16]{1,0:T(8,128)S(1)} %get-tuple-element.48), channel_id=1, replica_groups=mesh['head'=4,'seq'=8] {'seq'}, use_global_device_ids=true, to_apply=%region_5.6 | all-reduce | flops 128 | bytes 1024 | tf_op jit(solution)/shard_map/psum | solution.py:55
  79.1 0.3 fusion.2
  79.5 0.3 fusion.4
  79.8 0.9 copy.16
  80.7 0.0 reduce-scatter.4.cloned.1.call-update
  80.7 22.9 %reduce-scatter.4.cloned.1.call-done = bf16[64,576]{1,0:T(8,128)(2,1)} async-done(((bf16[256,576]{1,0:T(8,128)(2,1)}), bf16[64,576]{1,0:T(8,128)(2,1)}) %reduce-scatter.4.cloned.1.call-update) | async-done | bytes 73744 | tf_op jit(solution)/shard_map/reduce_scatter | solution.py:66
  103.6 9.2 %all_gather.23 = bf16[256,576]{1,0:T(8,128)(2,1)S(1)} all-gather(bf16[64,576]{1,0:T(8,128)(2,1)} %reduce-scatter.4.cloned.1.call-done), channel_id=1, replica_groups=mesh['head'=4,'seq'=8] {'head'}, dimensions={0}, use_global_device_ids=true | all-gather | bytes 368640 | tf_op jit(solution)/shard_map/all_gather | solution.py:78
  112.8 1.0 copy.13
  113.7 0.0 copy-done
  113.7 1.8 %convolution_convert_fusion = bf16[256,1792]{1,0:T(8,128)(2,1)} fusion(bf16[256,576]{1,0:T(8,128)(2,1)S(1)} %all_gather.23, bf16[1792,576]{0,1:T(8,128)(2,1)S(1)} %copy-done), kind=kOutput, calls=%fused_computation.5 | convolution fusion | flops 528941056 | bytes 3276800 | tf_op jit(solution)/shard_map/dot_general | solution.py:81
  (16 shorter events, 0.2 us)
Async XLA Ops:
  7.2 106.6 %copy-start = (bf16[1792,576]{0,1:T(8,128)(2,1)S(1)}, bf16[1792,576]{0,1:T(8,128)(2,1)}, u32[]{:S(2)}) copy-start(bf16[1792,576]{0,1:T(8,128)(2,1)} %param.13) | copy-start | bytes 6193156
  8.7 22.8 %all-to-all-start = ((bf16[8,1,16,576]{3,2,1,0:T(8,128)(2,1)}), bf16[8,1,16,576]{3,2,1,0:T(8,128)(2,1)S(1)}, u32[]{:S(2)}, u32[]{:S(2)}) async-start(bf16[8,1,16,576]{3,2,1,0:T(8,128)(2,1)} %stack.2), calls=%async_computation | async-start | bytes 327680 | tf_op jit(solution)/shard_map/all_to_all | solution.py:11
  15.1 88.5 %reduce-scatter.4.cloned.1.call-start = ((), (), s32[]{:S(2)}) async-start(), calls=%async_computation.2 | async-start | bytes 409600 | tf_op jit(solution)/shard_map/reduce_scatter | solution.py:66
Sparse Core Ops, SparseCore 0:
  80.8 22.6 reduce-scatter.3
